TPU v7x, 128 devices: a whole 4x4x4 slice. The times are simulated.
128 devices in a mesh: tok: 4 (over z_lo, core), con: 4 (over x), out: 8 (over z_hi, y).
Axes of the slice: x: 4, y: 4, z: 4 (z_hi: 2, z_lo: 2; z = z_hi * 2 + z_lo), core: 2. Of those that a mesh axis runs over, the one named last changes fastest.
Arguments:
- tokens: bfloat16 [1024, 10240], P('tok', 'con'), may hold values from -6 to 6
- out_grad: bfloat16 [1024, 10240], P('tok', 'con'), may hold values from -3 to 3
- weight_in: bfloat16 [10240, 20480], P('con', ('tok', 'out')), may hold values from -0.0625 to 0.0625
- weight_out: bfloat16 [20480, 10240], P(('tok', 'out'), 'con'), may hold values from -0.0390625 to 0.0390625
Outputs:
- input_grad: bfloat16 [1024, 10240], P(('tok', 'out'), 'con')
- first_grad: float32 [10240, 20480], P('con', ('tok', 'out'))
- second_grad: float32 [20480, 10240], P(('tok', 'out'), 'con')
All inputs are finite; a program needn't handle non-finite values.
Results may differ from a plain program's by a relative error of at most 0.0049.
Values may be sent and summed in bfloat16 or wider, within the bound.
No kernel may reach another device: no remote copies, remote signals or barrier semaphores. Data moves between devices by JAX's collectives and lax.ppermute only.
A program may use at most 128 MiB of HBM per device.

v0:
```python
import jax
import jax.numpy as jnp
from jax import lax
from jax.sharding import PartitionSpec as P


def gelu_parts(pre, act_grad):
    cdf = 0.5 * (1.0 + jax.scipy.special.erf(pre * 0.7071067811865476))
    density = jnp.exp(-0.5 * pre * pre) * 0.3989422804014327
    activ = (pre * cdf).astype(jnp.bfloat16)
    pre_grad = (act_grad * (cdf + pre * density)).astype(jnp.bfloat16)
    return (activ, pre_grad)


def per_device(tokens, out_grad, weight_in, weight_out):
    gathered_tok, gathered_grad = (
        lax.all_gather(tokens, "tok", axis=0, tiled=True),
        lax.all_gather(out_grad, "tok", axis=0, tiled=True),
    )
    pre_part = jnp.dot(gathered_tok, weight_in, preferred_element_type=jnp.float32)
    grad_part = lax.dot_general(
        gathered_grad, weight_out, (((1,), (1,)), ((), ())), preferred_element_type=jnp.float32
    )
    pre, act_grad = lax.psum((pre_part, grad_part), "con")
    activ, pre_grad = gelu_parts(pre, act_grad)
    first_grad = lax.dot_general(
        gathered_tok, pre_grad, (((0,), (0,)), ((), ())), preferred_element_type=jnp.float32
    )
    second_grad = lax.dot_general(
        activ, gathered_grad, (((0,), (0,)), ((), ())), preferred_element_type=jnp.float32
    )
    summed = lax.psum_scatter(
        lax.dot_general(
            pre_grad, weight_in, (((1,), (1,)), ((), ())), preferred_element_type=jnp.float32
        ),
        ("tok", "out"),
        scatter_dimension=0,
        tiled=True,
    )
    return (summed.astype(jnp.bfloat16), first_grad, second_grad)


def solution(mesh):
    placed = (P("tok", "con"), P("tok", "con"), P("con", ("tok", "out")), P(("tok", "out"), "con"))
    return jax.shard_map(
        per_device,
        mesh=mesh,
        in_specs=placed,
        out_specs=(P(("tok", "out"), "con"), P("con", ("tok", "out")), P(("tok", "out"), "con")),
        check_vma=False,
    )
```

profile of v0, /device:TPU:26, one launch (start us, length us, event | category | flops | bytes accessed | tf_op | source)
XLA Modules:
  0.0 438.6 jit_solution(11786640155277822944)
XLA Ops:
  7.2 0.0 copy-start
  7.2 0.0 all-gather.3.cloned.1.call-start
  7.2 0.7 all-gather.3.cloned.1.call-update
  7.9 0.0 all-gather.5.cloned.1.call-start
  8.0 0.7 all-gather.5.cloned.1.call-update
  8.7 0.0 all-reduce.3.cloned.1.call-start
  8.7 57.5 %all-gather.3.cloned.1.call-done = bf16[1024,2560]{1,0:T(8,128)(2,1)} async-done(((bf16[256,2560]{1,0:T(8,128)(2,1)}), bf16[1024,2560]{1,0:T(8,128)(2,1)}) %all-gather.3.cloned.1.call-update) | async-done | bytes 5242896 | tf_op jit(solution)/shard_map/all_gather | solution.py:18
  66.2 9.2 %fusion.7 = f32[1024,640]{1,0:T(8,128)} fusion(bf16[1024,2560]{1,0:T(8,128)(2,1)} %all-gather.3.cloned.1.call-done, bf16[640,2560]{1,0:T(8,128)(2,1)} %param.7), kind=kOutput, calls=%fused_computation.11 | convolution fusion | flops 3355443200 | bytes 11141120 | tf_op jit(solution)/shard_map/dot_general | solution.py:21
  75.4 48.6 %all-gather.5.cloned.1.call-done = bf16[1024,2560]{1,0:T(8,128)(2,1)} async-done(((bf16[256,2560]{1,0:T(8,128)(2,1)}), bf16[1024,2560]{1,0:T(8,128)(2,1)}) %all-gather.5.cloned.1.call-update) | async-done | bytes 5242896 | tf_op jit(solution)/shard_map/all_gather | solution.py:17
  124.0 0.0 copy-done
  124.0 8.2 %fusion.8 = f32[1024,640]{1,0:T(8,128)} fusion(bf16[1024,2560]{1,0:T(8,128)(2,1)} %all-gather.5.cloned.1.call-done, bf16[2560,640]{1,0:T(8,128)(2,1)S(1)} %copy-done), kind=kOutput, calls=%fused_computation.12 | convolution fusion | flops 3355443200 | bytes 11141120 | tf_op jit(solution)/shard_map/dot_general | solution.py:20
  132.2 0.0 all-reduce.3.cloned.1.call-update
  132.3 0.2 reduce-scatter.2.cloned.1.call-start
  132.5 110.4 %all-reduce.3.cloned.1.call-done = (f32[1024,640]{1,0:T(8,128)}, f32[1024,640]{1,0:T(8,128)}) async-done(((f32[1024,640]{1,0:T(8,128)}, f32[1024,640]{1,0:T(8,128)}), (f32[1024,640]{1,0:T(8,128)}, f32[1024,640]{1,0:T(8,128)})) %all-reduce.3.cloned.1.call-update) | async-done | bytes 5242896 | tf_op jit(solution)/shard_map/psum | solution.py:24
  242.9 3.1 fusion.5
  245.9 0.0 copy-start.1
  246.0 1.0 copy-done.1
  247.0 6.9 %fusion.9 = f32[1024,2560]{1,0:T(8,128)} fusion(bf16[1024,640]{1,0:T(8,128)(2,1)S(1)} %fusion.5, bf16[2560,640]{1,0:T(8,128)(2,1)S(1)} %copy-done), kind=kOutput, calls=%fused_computation.13 | convolution fusion | flops 3355443200 | bytes 15073280 | tf_op jit(solution)/shard_map/dot_general | solution.py:33
  253.9 0.0 reduce-scatter.2.cloned.1.call-update
  254.0 9.3 %convolution_bitcast_fusion = f32[2560,640]{0,1:T(8,128)} fusion(bf16[1024,640]{1,0:T(8,128)(2,1)} %copy-done.1, bf16[1024,2560]{1,0:T(8,128)(2,1)} %all-gather.5.cloned.1.call-done), kind=kOutput, calls=%fused_computation | convolution fusion | flops 3355443200 | bytes 13107200 | tf_op jit(solution)/shard_map/dot_general | solution.py:26
  263.2 8.3 %copy.7 = f32[2560,640]{1,0:T(8,128)} copy(f32[2560,640]{0,1:T(8,128)} %convolution_bitcast_fusion) | data formatting | bytes 13107200
  271.5 9.7 %fusion.6 = f32[640,2560]{1,0:T(8,128)} fusion(bf16[1024,2560]{1,0:T(8,128)(2,1)} %all-gather.3.cloned.1.call-done, f32[1024,640]{1,0:T(8,128)} %get-tuple-element.7), kind=kOutput, calls=%fused_computation.10 | convolution fusion | flops 3358720000 | bytes 14417920 | tf_op jit(solution)/shard_map/dot_general | solution.py:29
  281.2 149.2 %reduce-scatter.2.cloned.1.call-done = f32[32,2560]{1,0:T(8,128)} async-done(((f32[1024,2560]{1,0:T(8,128)}), f32[32,2560]{1,0:T(8,128)}) %reduce-scatter.2.cloned.1.call-update) | async-done | bytes 327696 | tf_op jit(solution)/shard_map/reduce_scatter | solution.py:32
  430.4 1.7 convert_element_type.10
Async XLA Ops:
  7.2 116.9 %copy-start = (bf16[2560,640]{1,0:T(8,128)(2,1)S(1)}, bf16[2560,640]{1,0:T(8,128)(2,1)}, u32[]{:S(2)}) copy-start(bf16[2560,640]{1,0:T(8,128)(2,1)} %param.6) | copy-start | bytes 9830404
  7.2 59.0 %all-gather.3.cloned.1.call-start = ((), (), s32[]{:S(2)}) async-start(), calls=%async_computation.1 | async-start | bytes 6553600 | tf_op jit(solution)/shard_map/all_gather | solution.py:18
  7.9 116.1 %all-gather.5.cloned.1.call-start = ((), (), s32[]{:S(2)}) async-start(), calls=%async_computation.2 | async-start | bytes 6553600 | tf_op jit(solution)/shard_map/all_gather | solution.py:17
  8.7 234.2 %all-reduce.3.cloned.1.call-start = ((), (), s32[]{:S(2)}) async-start(), calls=%async_computation.4 | async-start | bytes 10485760 | tf_op jit(solution)/shard_map/psum | solution.py:24
  132.3 298.1 %reduce-scatter.2.cloned.1.call-start = ((), (), s32[]{:S(2)}) async-start(), calls=%async_computation.3 | async-start | bytes 10813440 | tf_op jit(solution)/shard_map/reduce_scatter | solution.py:32
  245.9 1.1 copy-start.1
Sparse Core Ops, SparseCore 0:
  9.6 56.4 all-gather.2
  67.8 56.1 all-gather.4
  132.4 110.4 all-reduce.2
  254.1 176.2 reduce-scatter.1
where the time goes:
time: 439 us
  waiting for transfers between devices  367 us (84%)
  matrix products  43.4 us (10%)
  between operations  13.8 us (3%)
  local copies, waits for them, and re-layouts  9.32 us (2%)
  other arithmetic  4.71 us (1%)
    reduce_scatter x1, waiting for transfers between devices, per_device(): lax.psum_scatter(lax.dot_general(pre_grad, weight_in, (((1,), (1,)), ((),...  149 us
    psum x1, waiting for transfers between devices, per_device(): pre, act_grad = lax.psum((pre_part, grad_part), 'con')  110 us
    all_gather x1, waiting for transfers between devices, per_device(): lax.all_gather(out_grad, 'tok', axis=0, tiled=True)  57.5 us
    all_gather x1, waiting for transfers between devices, per_device(): lax.all_gather(tokens, 'tok', axis=0, tiled=True)  48.6 us
    dot_general x1, matrix products, per_device(): lax.dot_general(activ, gathered_grad, (((0,), (0,)), ((), ())), preferred...  9.72 us
    unnamed x5, local copies, waits for them, and re-layouts  9.32 us
    dot_general x1, matrix products, per_device(): lax.dot_general(gathered_tok, pre_grad, (((0,), (0,)), ((), ())), preferr...  9.29 us
    dot_general x1, matrix products, per_device(): lax.dot_general(gathered_grad, weight_out, (((1,), (1,)), ((), ())), pref...  9.24 us
  transfers between devices with their start and end apart: 4, of which 4 were waited for; matrix products, arithmetic and copies ran while one was open for 8% of the time, Pallas kernels for 0%

commit v1 on v0

--- a/solution.py
+++ b/solution.py
@@ -14,7 +14,9 @@
 
 def per_device(tokens, out_grad, weight_in, weight_out):
     gathered_tok, gathered_grad = (
-        lax.all_gather(tokens, "tok", axis=0, tiled=True),
+        jnp.concatenate(
+            lax.all_to_all(jnp.stack([tokens] * lax.axis_size("tok")), "tok", 0, 0), axis=0
+        ),
         lax.all_gather(out_grad, "tok", axis=0, tiled=True),
     )
     pre_part = jnp.dot(gathered_tok, weight_in, preferred_element_type=jnp.float32)

time: 439 us -> 438 us (level)
  waiting for transfers between devices: 367 us -> 258 us
  blocking collectives: 0 us -> 104 us
  local copies, waits for them, and re-layouts: 9.32 us -> 14.8 us
    all_to_all x0 -> x1, blocking collectives: none -> 104 us  [per_device(): lax.all_to_all(jnp.stack([tokens] * lax.axis_size('tok')), 'tok', 0, 0)]
    all_gather x1, waiting for transfers between devices: 57.5 us -> 0.01 us  [per_device(): lax.all_gather(out_grad, 'tok', axis=0, tiled=True)]
    all_gather x1 -> x0, waiting for transfers between devices: 48.6 us -> none  [per_device(): lax.all_gather(tokens, 'tok', axis=0, tiled=True)]
    unnamed x5 -> x11, local copies, waits for them, and re-layouts: 9.32 us -> 12.9 us
  transfers between devices with their start and end apart: 4 -> 3, of which waited for: 4 -> 2; matrix products, arithmetic and copies ran while one was open for 8% -> 8% of each run, Pallas kernels for 0% -> 0%
where the time goes in v1:
time: 438 us; the launch traced here: 436 us
  waiting for transfers between devices  258 us (59%)
  blocking collectives  104 us (24%)
  matrix products  40.7 us (9%)
  local copies, waits for them, and re-layouts  14.8 us (3%)
  between operations  13.8 us (3%)
  other arithmetic  4.71 us (1%)
    reduce_scatter x1, waiting for transfers between devices, per_device(): lax.psum_scatter(lax.dot_general(pre_grad, weight_in, (((1,), (1,)), ((),...  147 us
    psum x1, waiting for transfers between devices, per_device(): pre, act_grad = lax.psum((pre_part, grad_part), 'con')  110 us
    all_to_all x1, blocking collectives, per_device(): lax.all_to_all(jnp.stack([tokens] * lax.axis_size('tok')), 'tok', 0, 0)  104 us
    unnamed x11, local copies, waits for them, and re-layouts  12.9 us
    dot_general x1, matrix products, per_device(): lax.dot_general(activ, gathered_grad, (((0,), (0,)), ((), ())), preferred...  9.87 us
    dot_general x1, matrix products, per_device(): lax.dot_general(gathered_grad, weight_out, (((1,), (1,)), ((), ())), pref...  9.24 us
    dot_general x1, matrix products, per_device(): lax.dot_general(gathered_tok, pre_grad, (((0,), (0,)), ((), ())), preferr...  8.88 us
  transfers between devices with their start and end apart: 3, of which 2 were waited for; matrix products, arithmetic and copies ran while one was open for 8% of the time, Pallas kernels for 0%

profile of v1, /device:TPU:26, one launch (start us, length us, event | category | flops | bytes accessed | tf_op | source)
XLA Modules:
  0.0 436.3 jit_solution(2214214561377529420)
XLA Ops:
  7.2 0.0 copy-start
  7.2 0.0 all-gather.2.cloned.1.call-start
  7.2 0.7 all-gather.2.cloned.1.call-update
  7.9 0.0 all-reduce.3.cloned.1.call-start
  8.0 1.9 stack.2
  9.9 104.5 %all_to_all.5 = bf16[4,256,2560]{2,1,0:T(8,128)(2,1)S(1)} all-to-all(bf16[4,256,2560]{2,1,0:T(8,128)(2,1)S(1)} %stack.2), channel_id=1, replica_groups=mesh['tok'=4,'con'=4,'out'=8] {'tok'}, dimensions={0} | all-to-all | bytes 10485760 | tf_op jit(solution)/shard_map/all_to_all | solution.py:18
  114.4 2.4 copy-done.2
  116.7 0.0 copy-done
  116.7 5.8 %fusion.8 = f32[1024,640]{1,0:T(8,128)} fusion(bf16[1024,2560]{1,0:T(8,128)(2,1)S(1)} %bitcast.12, bf16[2560,640]{1,0:T(8,128)(2,1)S(1)} %copy-done), kind=kOutput, calls=%fused_computation.12 | convolution fusion | flops 3355443200 | bytes 11141120 | tf_op jit(solution)/shard_map/dot_general | solution.py:22
  122.5 9.2 %fusion.7 = f32[1024,640]{1,0:T(8,128)} fusion(bf16[1024,2560]{1,0:T(8,128)(2,1)} %all-gather.2.cloned.1.call-done, bf16[640,2560]{1,0:T(8,128)(2,1)} %param.7), kind=kOutput, calls=%fused_computation.11 | convolution fusion | flops 3355443200 | bytes 11141120 | tf_op jit(solution)/shard_map/dot_general | solution.py:23
  131.7 0.0 all-reduce.3.cloned.1.call-update
  131.8 0.2 reduce-scatter.2.cloned.1.call-start
  132.0 110.3 %all-reduce.3.cloned.1.call-done = (f32[1024,640]{1,0:T(8,128)}, f32[1024,640]{1,0:T(8,128)}) async-done(((f32[1024,640]{1,0:T(8,128)}, f32[1024,640]{1,0:T(8,128)}), (f32[1024,640]{1,0:T(8,128)}, f32[1024,640]{1,0:T(8,128)})) %all-reduce.3.cloned.1.call-update) | async-done | bytes 5242896 | tf_op jit(solution)/shard_map/psum | solution.py:26
  242.2 3.1 fusion.5
  245.3 0.0 copy-start.3
  245.3 1.0 copy-done.3
  246.4 6.9 %fusion.9 = f32[1024,2560]{1,0:T(8,128)} fusion(bf16[1024,640]{1,0:T(8,128)(2,1)S(1)} %fusion.5, bf16[2560,640]{1,0:T(8,128)(2,1)S(1)} %copy-done), kind=kOutput, calls=%fused_computation.13 | convolution fusion | flops 3355443200 | bytes 15073280 | tf_op jit(solution)/shard_map/dot_general | solution.py:35
  253.3 0.0 reduce-scatter.2.cloned.1.call-update
  253.3 1.3 copy-done.4
  254.6 8.9 %convolution_bitcast_fusion = f32[2560,640]{0,1:T(8,128)} fusion(bf16[1024,640]{1,0:T(8,128)(2,1)S(1)} %copy-done.4, bf16[1024,2560]{1,0:T(8,128)(2,1)} %bitcast.13), kind=kOutput, calls=%fused_computation | convolution fusion | flops 3355443200 | bytes 13107200 | tf_op jit(solution)/shard_map/dot_general | solution.py:28
  263.5 8.1 %copy.7 = f32[2560,640]{1,0:T(8,128)} copy(f32[2560,640]{0,1:T(8,128)} %convolution_bitcast_fusion) | data formatting | bytes 13107200
  271.6 9.9 %fusion.6 = f32[640,2560]{1,0:T(8,128)} fusion(bf16[1024,2560]{1,0:T(8,128)(2,1)} %all-gather.2.cloned.1.call-done, f32[1024,640]{1,0:T(8,128)} %get-tuple-element.7), kind=kOutput, calls=%fused_computation.10 | convolution fusion | flops 3358720000 | bytes 14417920 | tf_op jit(solution)/shard_map/dot_general | solution.py:31
  281.5 146.7 %reduce-scatter.2.cloned.1.call-done = f32[32,2560]{1,0:T(8,128)} async-done(((f32[1024,2560]{1,0:T(8,128)}), f32[32,2560]{1,0:T(8,128)}) %reduce-scatter.2.cloned.1.call-update) | async-done | bytes 327696 | tf_op jit(solution)/shard_map/reduce_scatter | solution.py:34
  428.2 1.7 convert_element_type.10
  (5 shorter events, 0.0 us)
Async XLA Ops:
  7.2 109.6 %copy-start = (bf16[2560,640]{1,0:T(8,128)(2,1)S(1)}, bf16[2560,640]{1,0:T(8,128)(2,1)}, u32[]{:S(2)}) copy-start(bf16[2560,640]{1,0:T(8,128)(2,1)} %param.6) | copy-start | bytes 9830404
  7.2 115.3 %all-gather.2.cloned.1.call-start = ((), (), s32[]{:S(2)}) async-start(), calls=%async_computation.2 | async-start | bytes 6553600 | tf_op jit(solution)/shard_map/all_gather | solution.py:20
  7.9 234.3 %all-reduce.3.cloned.1.call-start = ((), (), s32[]{:S(2)}) async-start(), calls=%async_computation.4 | async-start | bytes 10485760 | tf_op jit(solution)/shard_map/psum | solution.py:26
  114.4 2.4 copy-start.2
  131.8 296.4 %reduce-scatter.2.cloned.1.call-start = ((), (), s32[]{:S(2)}) async-start(), calls=%async_computation.3 | async-start | bytes 10813440 | tf_op jit(solution)/shard_map/reduce_scatter | solution.py:34
  245.3 1.1 copy-start.3
  253.3 1.3 copy-start.4
  271.6 158.2 %copy-start.1 = (bf16[2560,640]{1,0:T(8,128)(2,1)S(1)}, bf16[2560,640]{1,0:T(8,128)(2,1)}, u32[]{:S(2)}) copy-start(bf16[2560,640]{1,0:T(8,128)(2,1)} %param.6) | copy-start | bytes 9830404
Sparse Core Ops, SparseCore 0:
  9.6 99.4 all-gather.1
  131.9 110.3 all-reduce.2
  253.4 174.6 reduce-scatter.1
